TPU v7x, 512 devices: a whole 4x8x8 slice. The times are simulated.
512 devices in a mesh: item: 2 (over core), row: 16 (over y, z_lo), col: 16 (over z_hi, x).
Axes of the slice: x: 4, y: 8, z: 8 (z_hi: 4, z_lo: 2; z = z_hi * 2 + z_lo), core: 2. Of those that a mesh axis runs over, the one named last changes fastest.
Arguments:
- latents: bfloat16 [2, 2, 64, 64, 3072], P('item', None, 'row', 'col'), may hold values from -640 to 640
- prompt_rows: bfloat16 [2, 226, 3072], P('item'), may hold values from -640 to 640
- peg_weight: bfloat16 [3, 3, 3072], replicated, may hold values from -1 to 1
- modulation_weight: bfloat16 [512, 6144], P(None, 'col'), may hold values from -0.5 to 0.5
- qkv_weight: bfloat16 [3072, 3, 2048], P(('item', 'row'), None, 'col'), may hold values from -3 to 3
- text_len: int32 [2], P('item'), may hold values from 56 to 226, as said below
- timestep: int32 [2], P('item'), may hold values from 0 to 999
Outputs:
- attended: bfloat16 [2, 2, 64, 64, 2048], P('item', None, 'row', None, 'col')
Inputs may be any that keep to these rules, and one draw needn't show every extreme that they name: `text_len`: one item has all 226 text tokens valid; the others have fewer.
All inputs are finite; a program needn't handle non-finite values.
Results may differ from a plain program's by a relative error of at most 0.02.
Values may be sent and summed in bfloat16 or wider, within the bound.
No kernel may reach another device: no remote copies, remote signals or barrier semaphores. Data moves between devices by JAX's collectives and lax.ppermute only.
A program may use at most 64 MiB of HBM per device.

v0:
```python
import math
import jax
import jax.numpy as jnp
from jax import lax
from jax.sharding import PartitionSpec as P

HD = 64


def with_halo(block, sides, width):
    for axis, dim in sides:
        count = lax.axis_size(axis)
        forward = [(i, i + 1) for i in range(count - 1)]
        backward = [(target, source) for source, target in forward]
        low = lax.ppermute(
            lax.slice_in_dim(block, block.shape[dim] - width, None, axis=dim), axis, forward
        )
        high = lax.ppermute(lax.slice_in_dim(block, 0, width, axis=dim), axis, backward)
        block = jnp.concatenate([low, block, high], axis=dim)
    return block


def time_angles(step, count):
    half = count // 2
    freqs = jnp.exp(-math.log(10000.0) * jnp.arange(half, dtype=jnp.float32) / half)
    angle = step.astype(jnp.float32) * freqs
    return jnp.concatenate([jnp.cos(angle), jnp.sin(angle)])


def modulate(rows, shift, scale):
    values = rows.astype(jnp.float32)
    center = jnp.mean(values, axis=-1, keepdims=True)
    centered = values - center
    spread = jnp.mean(centered * centered, axis=-1, keepdims=True)
    return (centered * lax.rsqrt(spread + 1e-06) * (1.0 + scale) + shift).astype(jnp.bfloat16)


def absorb(carry, queries, key_rows, value_rows, valid):
    running_max, running_sum, weighted = carry
    count = key_rows.shape[0]
    heads = queries.shape[1]
    key_heads = key_rows.reshape(count, heads, HD)
    value_heads = value_rows.reshape(count, heads, HD)
    scores = (
        jnp.einsum("rhd,bhd->rhb", queries, key_heads, preferred_element_type=jnp.float32) * 0.125
    )
    if valid is not None:
        scores = jnp.where(valid[None, None, :], scores, -jnp.inf)
    newest = jnp.maximum(running_max, jnp.max(scores, axis=-1))
    weights = jnp.exp(scores - newest[..., None])
    shrink_by = jnp.exp(running_max - newest)
    running_sum = running_sum * shrink_by + jnp.sum(weights, axis=-1)
    weighted = weighted * shrink_by[..., None] + jnp.einsum(
        "rhb,bhd->rhd",
        weights.astype(jnp.bfloat16),
        value_heads,
        preferred_element_type=jnp.float32,
    )
    return (newest, running_sum, weighted)


def on_device(latents, prompt_rows, peg_weight, modulation_weight, qkv_weight, text_len, timestep):
    tile_h = latents.shape[2]
    tile_w = latents.shape[3]
    width = latents.shape[4]
    padded = with_halo(latents, (("row", 2), ("col", 3)), 1)
    summed = latents.astype(jnp.float32)
    for row_tap in range(3):
        for col_tap in range(3):
            summed = summed + padded[
                :, :, row_tap : row_tap + tile_h, col_tap : col_tap + tile_w, :
            ].astype(jnp.float32) * peg_weight[row_tap, col_tap].astype(jnp.float32)
    convolved = summed.astype(jnp.bfloat16)
    activation = jax.nn.silu(time_angles(timestep[0], modulation_weight.shape[0])).astype(
        jnp.bfloat16
    )
    own_columns = jnp.dot(
        activation[None, :], modulation_weight, preferred_element_type=jnp.float32
    )
    modulation = lax.all_gather(own_columns, "col", axis=1, tiled=True)[0]
    shift = modulation[:width]
    scale = modulation[width:]
    group_rows = lax.all_gather(modulate(convolved, shift, scale), "col", axis=3, tiled=True)
    frames = group_rows.shape[1]
    grid_w = group_rows.shape[3]
    flat_rows = group_rows.reshape(-1, width)
    row_count = flat_rows.shape[0]
    text_normed = modulate(prompt_rows[0], shift, scale)
    text_count = text_normed.shape[0]
    head_width = qkv_weight.shape[2]
    full_weight = lax.all_gather(qkv_weight, ("item", "row"), axis=0, tiled=True)
    latent_proj = jnp.einsum(
        "rd,dkc->rkc", flat_rows, full_weight, preferred_element_type=jnp.float32
    )
    text_proj = jnp.einsum(
        "rd,dkc->rkc", text_normed, full_weight, preferred_element_type=jnp.float32
    )
    latent_qkv = latent_proj.astype(jnp.bfloat16)
    text_qkv = text_proj.astype(jnp.bfloat16)
    heads = head_width // HD
    queries = latent_qkv[:, 0, :].reshape(row_count, heads, HD)
    local_keys = latent_qkv[:, 1, :]
    local_values = latent_qkv[:, 2, :]
    text_valid = jnp.arange(text_count, dtype=jnp.int32) < text_len[0]
    start_carry = (
        jnp.full((row_count, heads), -jnp.inf, jnp.float32),
        jnp.zeros((row_count, heads), jnp.float32),
        jnp.zeros((row_count, heads, HD), jnp.float32),
    )
    text_carry = absorb(start_carry, queries, text_qkv[:, 1, :], text_qkv[:, 2, :], text_valid)
    key_rows = lax.all_gather(local_keys, "row", axis=0, tiled=True)
    value_rows = lax.all_gather(local_values, "row", axis=0, tiled=True)
    total_rows = key_rows.shape[0]
    block_count = total_rows // row_count

    def one_block(state, pair):
        return (absorb(state, queries, pair[0], pair[1], None), None)

    state, unused = lax.scan(
        one_block,
        text_carry,
        (
            key_rows.reshape(block_count, row_count, head_width),
            value_rows.reshape(block_count, row_count, head_width),
        ),
    )
    running_max, running_sum, weighted = state
    attended = (weighted / running_sum[..., None]).astype(jnp.bfloat16)
    return attended.reshape(1, frames, tile_h, grid_w, head_width)


def solution(mesh):
    in_specs = (
        P("item", None, "row", "col", None),
        P("item", None, None),
        P(),
        P(None, "col"),
        P(("item", "row"), None, "col"),
        P("item"),
        P("item"),
    )
    out_specs = P("item", None, "row", None, "col")
    return jax.shard_map(
        on_device, mesh=mesh, in_specs=in_specs, out_specs=out_specs, check_vma=False
    )
```

profile of v0, /device:TPU:6, one launch (start us, length us, event | category | flops | bytes accessed | tf_op | source)
XLA Modules:
  0.0 427.7 jit_solution(11197046939042537317)
XLA Ops:
  6.5 1.1 copy.22
  7.8 1.3 collective-permute-start.1
  9.1 4.9 %collective-permute-start = (bf16[1,2,1,4,3072]{4,2,1,0,3:T(2,128)(2,1)S(1)}, bf16[1,2,1,4,3072]{4,2,1,0,3:T(2,128)(2,1)S(1)}, u32[]{:S(2)}, u32[]{:S(2)}) collective-permute-start(bf16[1,2,1,4,3072]{4,2,1,0,3:T(2,128)(2,1)S(1)} %get-tuple-element.95), channel_id=1, source_target_pairs={{0,16},{16,32},{32,48},{48,64},{64,80},{80,96},{96,112},{112,128},... | collective-permute-start | bytes 147464 | tf_op jit(solution)/shard_map/ppermute | solution.py:15
  14.7 1.0 slice_convert_fusion.8
  15.9 39.2 %all-gather.3 = f32[16,1,384]{2,1,0:T(1,128)S(1)} all-gather(f32[1,1,384]{2,1,0:T(1,128)S(1)} %convolution_bitcast_fusion.2), channel_id=2, replica_groups=mesh['item'=2,'row'=16,'col'=16] {'col'}, dimensions={0}, use_global_device_ids=true | all-gather | bytes 26112 | tf_op jit(solution)/shard_map/all_gather | solution.py:80
  55.2 6.1 %collective-permute-start.2 = (bf16[1,2,6,1,3072]{4,2,1,0,3:T(8,128)(2,1)S(1)}, bf16[1,2,6,1,3072]{4,2,1,0,3:T(8,128)(2,1)S(1)}, u32[]{:S(2)}, u32[]{:S(2)}) collective-permute-start(bf16[1,2,6,1,3072]{4,2,1,0,3:T(8,128)(2,1)S(1)} %get-tuple-element.93), channel_id=1, source_target_pairs={{0,1},{1,2},{2,3},{3,4},{4,5},{5,6},{6,7},{7,8},{8,9},{9,10},{10,1... | collective-permute-start | bytes 221192 | tf_op jit(solution)/shard_map/ppermute | solution.py:15
  61.4 3.1 collective-permute-start.3
  64.5 0.6 collective-permute-done.2
  65.1 5.7 %collective-permute-done.3 = bf16[1,2,6,1,3072]{4,2,1,0,3:T(8,128)(2,1)S(1)} collective-permute-done((bf16[1,2,6,1,3072]{4,2,1,0,3:T(8,128)(2,1)S(1)}, bf16[1,2,6,1,3072]{4,2,1,0,3:T(8,128)(2,1)S(1)}, u32[]{:S(2)}, u32[]{:S(2)}) %collective-permute-start.3) | collective-permute-done | bytes 73760 | tf_op jit(solution)/shard_map/ppermute | solution.py:18
  70.9 0.6 maximum_maximum_fusion
  71.5 1.4 convert_reduce_fusion.1
  73.1 0.9 fusion.37
  74.1 0.7 all-gather.9.cloned.1.call-update
  74.8 77.8 %all-gather.11.cloned.1.call-done = bf16[1,2,4,64,3072]{4,2,1,0,3:T(4,128)(2,1)} async-done(((bf16[1,2,4,4,3072]{4,2,1,0,3:T(4,128)(2,1)}), bf16[1,2,4,64,3072]{4,2,1,0,3:T(4,128)(2,1)}) %all-gather.11.cloned.1.call-update) | async-done | bytes 3145744 | tf_op jit(solution)/shard_map/all_gather | solution.py:83
  152.7 5.3 %copy.28 = bf16[1,2,4,64,3072]{4,3,2,1,0:T(8,128)(2,1)} copy(bf16[1,2,4,64,3072]{4,2,1,0,3:T(4,128)(2,1)} %all-gather.11.cloned.1.call-done) | data formatting | bytes 6291456 | tf_op jit(solution)/shard_map/all_gather | solution.py:83
  158.0 62.5 %all-gather.9.cloned.1.call-done = bf16[3072,3,128]{2,0,1:T(8,128)(2,1)} async-done(((bf16[96,3,128]{2,0,1:T(8,128)(2,1)}), bf16[3072,3,128]{2,0,1:T(8,128)(2,1)}) %all-gather.9.cloned.1.call-update) | async-done | bytes 2359312 | tf_op jit(solution)/shard_map/all_gather | solution.py:91
  220.5 4.1 convolution_convert_fusion
  224.6 0.7 fusion.52
  227.0 0.5 fusion.11
  227.6 1.1 fusion.24
  229.7 71.5 %all-gather.13.cloned.1.call-done = bf16[8192,1,128]{0,2,1:T(8,128)(2,1)} async-done(((bf16[512,1,128]{0,2,1:T(8,128)(2,1)}), bf16[8192,1,128]{0,2,1:T(8,128)(2,1)}) %all-gather.13.cloned.1.call-update) | async-done | bytes 2097168 | tf_op jit(solution)/shard_map/all_gather | solution.py:111
  301.2 2.4 copy.35
  303.6 1.2 copy.30
  304.8 72.2 %all-gather.15.cloned.1.call-done = bf16[8192,1,128]{0,2,1:T(8,128)(2,1)} async-done(((bf16[512,1,128]{0,2,1:T(8,128)(2,1)}), bf16[8192,1,128]{0,2,1:T(8,128)(2,1)}) %all-gather.15.cloned.1.call-update) | async-done | bytes 2097168 | tf_op jit(solution)/shard_map/all_gather | solution.py:112
  377.0 2.4 copy.36
  379.5 2.5 copy.31
  382.0 38.1 %while.14 = (s32[]{:T(128)}, f32[512,2]{0,1:T(2,128)S(1)}, f32[512,2]{0,1:T(2,128)S(1)}, f32[512,2,64]{0,2,1:T(8,128)S(1)}, bf16[16,512,128]{1,2,0:T(8,128)(2,1)...) while((s32[]{:T(128)}, f32[512,2]{0,1:T(2,128)S(1)}, ...), condition=%wide.region_9.10_spmd, body=%wide.region_6.9_spmd.sunk | while | flops 138545152 | bytes 7798881 | solution.py:119
  382.0 0.9 constant_dynamic-slice_fusion.3
  384.3 0.9 constant_dynamic-slice_fusion.3
  386.7 0.9 constant_dynamic-slice_fusion.3
  388.6 0.5 fusion.78
  389.1 0.9 constant_dynamic-slice_fusion.3
  391.5 0.9 constant_dynamic-slice_fusion.3
  393.9 0.9 constant_dynamic-slice_fusion.3
  396.2 0.9 constant_dynamic-slice_fusion.3
  398.1 0.5 fusion.78
  398.6 0.9 constant_dynamic-slice_fusion.3
  400.5 0.5 fusion.78
  401.0 0.9 constant_dynamic-slice_fusion.3
  402.9 0.5 fusion.78
  403.4 0.9 constant_dynamic-slice_fusion.3
  405.8 0.9 constant_dynamic-slice_fusion.3
  408.2 0.9 constant_dynamic-slice_fusion.3
  410.5 0.9 constant_dynamic-slice_fusion.3
  412.9 0.9 constant_dynamic-slice_fusion.3
  415.3 0.9 constant_dynamic-slice_fusion.3
  417.7 0.9 constant_dynamic-slice_fusion.3
  420.3 0.8 copy.34
  (130 shorter events, 23.6 us)
Async XLA Ops:
  6.5 9.2 %copy-start = (bf16[512,384]{1,0:T(8,128)(2,1)S(1)}, bf16[512,384]{1,0:T(8,128)(2,1)}, u32[]{:S(2)}) copy-start(bf16[512,384]{1,0:T(8,128)(2,1)} %param.12) | copy-start | bytes 1179652
  6.5 146.1 %all-gather.11.cloned.1.call-start = ((), (), s32[]{:S(2)}) async-start(), calls=%async_computation.1 | async-start | bytes 3342336 | tf_op jit(solution)/shard_map/all_gather | solution.py:83
  7.8 47.3 %collective-permute-start.1 = (bf16[1,2,1,4,3072]{4,2,1,0,3:T(2,128)(2,1)S(1)}, bf16[1,2,1,4,3072]{4,2,1,0,3:T(2,128)(2,1)S(1)}, u32[]{:S(2)}, u32[]{:S(2)}) collective-permute-start(bf16[1,2,1,4,3072]{4,2,1,0,3:T(2,128)(2,1)S(1)} %get-tuple-element.96), channel_id=1, source_target_pairs={{16,0},{32,16},{48,32},{64,48},{80,64},{96,80},{112,96},{128,112},... | collective-permute-start | bytes 147464 | tf_op jit(solution)/shard_map/ppermute | solution.py:18
  9.1 46.0 %collective-permute-start = (bf16[1,2,1,4,3072]{4,2,1,0,3:T(2,128)(2,1)S(1)}, bf16[1,2,1,4,3072]{4,2,1,0,3:T(2,128)(2,1)S(1)}, u32[]{:S(2)}, u32[]{:S(2)}) collective-permute-start(bf16[1,2,1,4,3072]{4,2,1,0,3:T(2,128)(2,1)S(1)} %get-tuple-element.95), channel_id=1, source_target_pairs={{0,16},{16,32},{32,48},{48,64},{64,80},{80,96},{96,112},{112,128},... | collective-permute-start | bytes 147464 | tf_op jit(solution)/shard_map/ppermute | solution.py:15
  55.2 9.9 %collective-permute-start.2 = (bf16[1,2,6,1,3072]{4,2,1,0,3:T(8,128)(2,1)S(1)}, bf16[1,2,6,1,3072]{4,2,1,0,3:T(8,128)(2,1)S(1)}, u32[]{:S(2)}, u32[]{:S(2)}) collective-permute-start(bf16[1,2,6,1,3072]{4,2,1,0,3:T(8,128)(2,1)S(1)} %get-tuple-element.93), channel_id=1, source_target_pairs={{0,1},{1,2},{2,3},{3,4},{4,5},{5,6},{6,7},{7,8},{8,9},{9,10},{10,1... | collective-permute-start | bytes 221192 | tf_op jit(solution)/shard_map/ppermute | solution.py:15
  61.4 9.5 %collective-permute-start.3 = (bf16[1,2,6,1,3072]{4,2,1,0,3:T(8,128)(2,1)S(1)}, bf16[1,2,6,1,3072]{4,2,1,0,3:T(8,128)(2,1)S(1)}, u32[]{:S(2)}, u32[]{:S(2)}) collective-permute-start(bf16[1,2,6,1,3072]{4,2,1,0,3:T(8,128)(2,1)S(1)} %get-tuple-element.94), channel_id=1, source_target_pairs={{1,0},{2,1},{3,2},{4,3},{5,4},{6,5},{7,6},{8,7},{9,8},{10,9},{11,1... | collective-permute-start | bytes 221192 | tf_op jit(solution)/shard_map/ppermute | solution.py:18
  74.0 146.4 %all-gather.9.cloned.1.call-start = ((), (), s32[]{:S(2)}) async-start(), calls=%async_computation | async-start | bytes 2433024 | tf_op jit(solution)/shard_map/all_gather | solution.py:91
  74.8 226.4 %all-gather.13.cloned.1.call-start = ((), (), s32[]{:S(2)}) async-start(), calls=%async_computation.2 | async-start | bytes 2228224 | tf_op jit(solution)/shard_map/all_gather | solution.py:111
  220.5 6.3 %copy-start.1 = (bf16[1,226,3072]{2,1,0:T(8,128)(2,1)S(1)}, bf16[1,226,3072]{2,1,0:T(8,128)(2,1)}, u32[]{:S(2)}) copy-start(bf16[1,226,3072]{2,1,0:T(8,128)(2,1)} %param.10) | copy-start | bytes 4165636
  225.4 151.7 %all-gather.15.cloned.1.call-start = ((), (), s32[]{:S(2)}) async-start(), calls=%async_computation.3 | async-start | bytes 2228224 | tf_op jit(solution)/shard_map/all_gather | solution.py:112
  225.9 1.7 copy-start.2
Sparse Core Ops, SparseCore 0:
  74.2 78.4 all-gather.10
  154.8 65.5 all-gather.8
  225.5 75.6 all-gather.12
  303.2 73.8 all-gather.14
where the time goes:
time: 428 us
  waiting for transfers between devices  291 us (68%)
  blocking collectives  39.2 us (9%)
  local copies, waits for them, and re-layouts  31.9 us (7%)
  matrix products  22.3 us (5%)
  starting transfers between devices  15.8 us (4%)
  between operations  14.8 us (3%)
  other arithmetic  11.6 us (3%)
    all_gather x1, waiting for transfers between devices, on_device(): lax.all_gather(modulate(convolved, shift, scale), 'col', axis=3, tiled=True)  77.8 us
    all_gather x1, waiting for transfers between devices, on_device(): value_rows = lax.all_gather(local_values, 'row', axis=0, tiled=True)  72.2 us
    all_gather x1, waiting for transfers between devices, on_device(): key_rows = lax.all_gather(local_keys, 'row', axis=0, tiled=True)  71.5 us
    all_gather x1, waiting for transfers between devices, on_device(): lax.all_gather(qkv_weight, ('item', 'row'), axis=0, tiled=True)  62.5 us
    all_gather x1, blocking collectives, on_device(): modulation = lax.all_gather(own_columns, 'col', axis=1, tiled=True)[0]  39.2 us
    dynamic_slice x16, local copies, waits for them, and re-layouts, on_device(): lax.scan(one_block, text_carry, (key_rows.reshape(block_count, row_count,...  14.8 us
    ppermute x2, starting transfers between devices, with_halo(): lax.ppermute(lax.slice_in_dim(block, block.shape[dim] - width, None, axis...  11 us
  transfers between devices with their start and end apart: 8, of which 6 were waited for; matrix products, arithmetic and copies ran while one was open for 3% of the time, Pallas kernels for 0%

commit v1 on v0

--- a/solution.py
+++ b/solution.py
@@ -80,7 +80,12 @@
     modulation = lax.all_gather(own_columns, "col", axis=1, tiled=True)[0]
     shift = modulation[:width]
     scale = modulation[width:]
-    group_rows = lax.all_gather(modulate(convolved, shift, scale), "col", axis=3, tiled=True)
+    group_rows = jnp.concatenate(
+        lax.all_to_all(
+            jnp.stack([modulate(convolved, shift, scale)] * lax.axis_size("col")), "col", 0, 0
+        ),
+        axis=3,
+    )
     frames = group_rows.shape[1]
     grid_w = group_rows.shape[3]
     flat_rows = group_rows.reshape(-1, width)

time: 428 us -> 380 us (0.89)
  waiting for transfers between devices: 291 us -> 226 us
  starting transfers between devices: 15.8 us -> 26.1 us
  local copies, waits for them, and re-layouts: 31.9 us -> 39.5 us
    all_gather x1 -> x0, waiting for transfers between devices: 77.8 us -> none  [on_device(): lax.all_gather(modulate(convolved, shift, scale), 'col', axis=3, tiled=True)]
    all_to_all x0 -> x1, waiting for transfers between devices: none -> 72.5 us  [on_device(): lax.all_to_all(jnp.stack([modulate(convolved, shift, scale)] * lax.axis_s...]
    all_gather x1, waiting for transfers between devices: 62.5 us -> 1.12 us  [on_device(): lax.all_gather(qkv_weight, ('item', 'row'), axis=0, tiled=True)]
    all_to_all x0 -> x1, starting transfers between devices: none -> 11.1 us  [on_device(): lax.all_to_all(jnp.stack([modulate(convolved, shift, scale)] * lax.axis_s...]
    another operation x0 -> x2, local copies, waits for them, and re-layouts: none -> 8.95 us  [the longest x1 5.9 us: on_device(): flat_rows = group_rows.reshape(-1, width)]
    all_gather x1 -> x0, local copies, waits for them, and re-layouts: 5.3 us -> none  [on_device(): lax.all_gather(modulate(convolved, shift, scale), 'col', axis=3, tiled=True)]
    ppermute x2, starting transfers between devices: 11 us -> 6.2 us  [with_halo(): lax.ppermute(lax.slice_in_dim(block, block.shape[dim] - width, None, axis...]
    ppermute x2, waiting for transfers between devices: 5.74 us -> 0.91 us  [with_halo(): lax.ppermute(lax.slice_in_dim(block, 0, width, axis=dim), axis, backward)]
  transfers between devices with their start and end apart: 8 -> 8, of which waited for: 6 -> 6; matrix products, arithmetic and copies ran while one was open for 3% -> 5% of each run, Pallas kernels for 0% -> 0%
where the time goes in v1:
time: 380 us; the launch traced here: 379 us
  waiting for transfers between devices  226 us (59%)
  local copies, waits for them, and re-layouts  39.5 us (10%)
  blocking collectives  38.8 us (10%)
  starting transfers between devices  26.1 us (7%)
  matrix products  22.2 us (6%)
  between operations  14.8 us (4%)
  other arithmetic  10.8 us (3%)
    all_gather x1, waiting for transfers between devices, on_device(): key_rows = lax.all_gather(local_keys, 'row', axis=0, tiled=True)  73.7 us
    all_to_all x1, waiting for transfers between devices, on_device(): lax.all_to_all(jnp.stack([modulate(convolved, shift, scale)] * lax.axis_s...  72.5 us
    all_gather x1, waiting for transfers between devices, on_device(): value_rows = lax.all_gather(local_values, 'row', axis=0, tiled=True)  72.4 us
    all_gather x1, blocking collectives, on_device(): modulation = lax.all_gather(own_columns, 'col', axis=1, tiled=True)[0]  38.8 us
    dynamic_slice x16, local copies, waits for them, and re-layouts, on_device(): lax.scan(one_block, text_carry, (key_rows.reshape(block_count, row_count,...  14.8 us
    all_to_all x1, starting transfers between devices, on_device(): lax.all_to_all(jnp.stack([modulate(convolved, shift, scale)] * lax.axis_s...  11.1 us
    dot_general x17, matrix products, absorb(): jnp.einsum('rhb,bhd->rhd', weights.astype(jnp.bfloat16), value_heads, pre...  8.55 us
    ppermute x2, starting transfers between devices, with_halo(): lax.ppermute(lax.slice_in_dim(block, 0, width, axis=dim), axis, backward)  8.46 us
  transfers between devices with their start and end apart: 8, of which 6 were waited for; matrix products, arithmetic and copies ran while one was open for 5% of the time, Pallas kernels for 0%

profile of v1, /device:TPU:6, one launch (start us, length us, event | category | flops | bytes accessed | tf_op | source)
XLA Modules:
  0.0 378.9 jit_solution(12872699704868458330)
XLA Ops:
  6.5 0.9 fusion.59
  7.5 4.3 %collective-permute-start = (bf16[1,2,1,4,3072]{4,3,2,1,0:T(4,128)(2,1)S(1)}, bf16[1,2,1,4,3072]{4,3,2,1,0:T(4,128)(2,1)S(1)}, u32[]{:S(2)}, u32[]{:S(2)}) collective-permute-start(bf16[1,2,1,4,3072]{4,3,2,1,0:T(4,128)(2,1)S(1)} %get-tuple-element.94), channel_id=1, source_target_pairs={{0,16},{16,32},{32,48},{48,64},{64,80},{80,96},{96,112},{112,128},... | collective-permute-start | bytes 147464 | tf_op jit(solution)/shard_map/ppermute | solution.py:15
  11.7 1.3 collective-permute-start.1
  13.8 1.0 slice_convert_fusion.8
  15.0 38.8 %all-gather.3 = f32[16,1,384]{2,1,0:T(1,128)S(1)} all-gather(f32[1,1,384]{2,1,0:T(1,128)S(1)} %convolution_bitcast_fusion.2), channel_id=2, replica_groups=mesh['item'=2,'row'=16,'col'=16] {'col'}, dimensions={0}, use_global_device_ids=true | all-gather | bytes 26112 | tf_op jit(solution)/shard_map/all_gather | solution.py:80
  53.8 1.0 constant_dynamic-update-slice_fusion.1
  55.0 7.2 %collective-permute-start.3 = (bf16[1,2,6,1,3072]{4,3,2,1,0:T(2,128)(2,1)S(1)}, bf16[1,2,6,1,3072]{4,3,2,1,0:T(2,128)(2,1)S(1)}, u32[]{:S(2)}, u32[]{:S(2)}) collective-permute-start(bf16[1,2,6,1,3072]{4,3,2,1,0:T(2,128)(2,1)S(1)} %get-tuple-element.92), channel_id=1, source_target_pairs={{1,0},{2,1},{3,2},{4,3},{5,4},{6,5},{7,6},{8,7},{9,8},{10,9},{11,1... | collective-permute-start | bytes 221192 | tf_op jit(solution)/shard_map/ppermute | solution.py:18
  62.2 1.9 collective-permute-start.2
  64.2 0.9 collective-permute-done.3
  65.1 4.2 %collective-permute-done.2 = bf16[1,2,6,1,3072]{4,3,2,1,0:T(2,128)(2,1)S(1)} collective-permute-done((bf16[1,2,6,1,3072]{4,3,2,1,0:T(2,128)(2,1)S(1)}, bf16[1,2,6,1,3072]{4,3,2,1,0:T(2,128)(2,1)S(1)}, u32[]{:S(2)}, u32[]{:S(2)}) %collective-permute-start.2) | collective-permute-done | bytes 73760 | tf_op jit(solution)/shard_map/ppermute | solution.py:15
  69.2 2.0 convert_reduce_fusion.1
  71.8 3.0 stack.2
  74.8 11.1 %all-to-all-start = ((bf16[16,1,2,4,4,3072]{5,4,3,2,1,0:T(4,128)(2,1)}), bf16[16,1,2,4,4,3072]{5,4,3,2,1,0:T(4,128)(2,1)S(1)}, u32[]{:S(2)}, u32[]{:S(2)}) async-start(bf16[16,1,2,4,4,3072]{5,4,3,2,1,0:T(4,128)(2,1)} %stack.2), calls=%async_computation | async-start | bytes 6291456 | tf_op jit(solution)/shard_map/all_to_all | solution.py:84
  86.0 0.7 all-gather.8.cloned.1.call-update
  86.7 72.5 %all-to-all-done = bf16[16,1,2,4,4,3072]{5,4,3,2,1,0:T(4,128)(2,1)S(1)} async-done(((bf16[16,1,2,4,4,3072]{5,4,3,2,1,0:T(4,128)(2,1)}), bf16[16,1,2,4,4,3072]{5,4,3,2,1,0:T(4,128)(2,1)S(1)}, u32[]{:S(2)}, u32[]{:S(2)}) %all-to-all-start) | async-done | bytes 3145760 | tf_op jit(solution)/shard_map/all_to_all | solution.py:84
  159.2 2.9 copy.22
  162.2 5.9 %reshape.200 = bf16[512,3072,1]{1,0,2:T(8,128)(2,1)} reshape(bf16[1,2,4,16,4,3072]{5,4,3,2,1,0:T(4,128)(2,1)} %copy.22) | data formatting | bytes 6291456 | tf_op jit(solution)/shard_map/reshape;reshape | solution.py:91
  168.1 1.1 all-gather.8.cloned.1.call-done
  169.2 4.0 %convolution_convert_fusion = bf16[512,3,128]{0,2,1:T(8,128)(2,1)S(1)} fusion(bf16[512,3072,1]{1,0,2:T(8,128)(2,1)} %reshape.200, bf16[3072,3,128]{2,0,1:T(8,128)(2,1)} %all-gather.8.cloned.1.call-done), kind=kOutput, calls=%fused_computation.32 | convolution fusion | flops 1208156160 | bytes 5898240 | tf_op jit(solution)/shard_map/rd,dkc->rkc/dot_general | solution.py:97
  173.3 0.7 fusion.57
  175.9 0.5 fusion.11
  176.4 1.1 fusion.24
  178.5 73.7 %all-gather.10.cloned.1.call-done = bf16[8192,1,128]{0,2,1:T(8,128)(2,1)} async-done(((bf16[512,1,128]{0,2,1:T(8,128)(2,1)}), bf16[8192,1,128]{0,2,1:T(8,128)(2,1)}) %all-gather.10.cloned.1.call-update) | async-done | bytes 2097168 | tf_op jit(solution)/shard_map/all_gather | solution.py:116
  252.3 2.4 copy.29
  254.7 1.2 copy.24
  255.9 72.4 %all-gather.12.cloned.1.call-done = bf16[8192,1,128]{0,2,1:T(8,128)(2,1)} async-done(((bf16[512,1,128]{0,2,1:T(8,128)(2,1)}), bf16[8192,1,128]{0,2,1:T(8,128)(2,1)}) %all-gather.12.cloned.1.call-update) | async-done | bytes 2097168 | tf_op jit(solution)/shard_map/all_gather | solution.py:117
  328.2 2.4 copy.30
  330.7 2.5 copy.25
  333.2 38.1 %while.14 = (s32[]{:T(128)}, f32[512,2]{0,1:T(2,128)S(1)}, f32[512,2]{0,1:T(2,128)S(1)}, f32[512,2,64]{0,2,1:T(8,128)S(1)}, bf16[16,512,128]{1,2,0:T(8,128)(2,1)...) while((s32[]{:T(128)}, f32[512,2]{0,1:T(2,128)S(1)}, ...), condition=%wide.region_9.10_spmd, body=%wide.region_6.9_spmd.sunk | while | flops 138545152 | bytes 7798881 | solution.py:124
  333.2 0.9 constant_dynamic-slice_fusion.3
  335.5 0.9 constant_dynamic-slice_fusion.3
  337.4 0.5 fusion.84
  337.9 0.9 constant_dynamic-slice_fusion.3
  339.8 0.5 fusion.84
  340.3 0.9 constant_dynamic-slice_fusion.3
  342.7 0.9 constant_dynamic-slice_fusion.3
  345.1 0.9 constant_dynamic-slice_fusion.3
  347.5 0.9 constant_dynamic-slice_fusion.3
  349.8 0.9 constant_dynamic-slice_fusion.3
  352.2 0.9 constant_dynamic-slice_fusion.3
  354.6 0.9 constant_dynamic-slice_fusion.3
  357.0 0.9 constant_dynamic-slice_fusion.3
  359.4 0.9 constant_dynamic-slice_fusion.3
  361.8 0.9 constant_dynamic-slice_fusion.3
  364.1 0.9 constant_dynamic-slice_fusion.3
  366.5 0.9 constant_dynamic-slice_fusion.3
  368.9 0.9 constant_dynamic-slice_fusion.3
  371.5 0.8 copy.28
  (138 shorter events, 24.9 us)
Async XLA Ops:
  6.5 8.2 %copy-start = (bf16[512,384]{1,0:T(8,128)(2,1)S(1)}, bf16[512,384]{1,0:T(8,128)(2,1)}, u32[]{:S(2)}) copy-start(bf16[512,384]{1,0:T(8,128)(2,1)} %param.12) | copy-start | bytes 1179652
  6.5 62.7 %copy-start.2 = (bf16[1,2,4,4,3072]{4,3,2,1,0:T(4,128)(2,1)S(1)}, bf16[1,2,4,4,3072]{4,3,2,1,0:T(4,128)(2,1)}, u32[]{:S(2)}) copy-start(bf16[1,2,4,4,3072]{4,3,2,1,0:T(4,128)(2,1)} %param.9) | copy-start | bytes 589828
  7.5 46.3 %collective-permute-start = (bf16[1,2,1,4,3072]{4,3,2,1,0:T(4,128)(2,1)S(1)}, bf16[1,2,1,4,3072]{4,3,2,1,0:T(4,128)(2,1)S(1)}, u32[]{:S(2)}, u32[]{:S(2)}) collective-permute-start(bf16[1,2,1,4,3072]{4,3,2,1,0:T(4,128)(2,1)S(1)} %get-tuple-element.94), channel_id=1, source_target_pairs={{0,16},{16,32},{32,48},{48,64},{64,80},{80,96},{96,112},{112,128},... | collective-permute-start | bytes 147464 | tf_op jit(solution)/shard_map/ppermute | solution.py:15
  11.7 43.0 %collective-permute-start.1 = (bf16[1,2,1,4,3072]{4,3,2,1,0:T(4,128)(2,1)S(1)}, bf16[1,2,1,4,3072]{4,3,2,1,0:T(4,128)(2,1)S(1)}, u32[]{:S(2)}, u32[]{:S(2)}) collective-permute-start(bf16[1,2,1,4,3072]{4,3,2,1,0:T(4,128)(2,1)S(1)} %get-tuple-element.93), channel_id=1, source_target_pairs={{16,0},{32,16},{48,32},{64,48},{80,64},{96,80},{112,96},{128,112},... | collective-permute-start | bytes 147464 | tf_op jit(solution)/shard_map/ppermute | solution.py:18
  55.0 10.0 %collective-permute-start.3 = (bf16[1,2,6,1,3072]{4,3,2,1,0:T(2,128)(2,1)S(1)}, bf16[1,2,6,1,3072]{4,3,2,1,0:T(2,128)(2,1)S(1)}, u32[]{:S(2)}, u32[]{:S(2)}) collective-permute-start(bf16[1,2,6,1,3072]{4,3,2,1,0:T(2,128)(2,1)S(1)} %get-tuple-element.92), channel_id=1, source_target_pairs={{1,0},{2,1},{3,2},{4,3},{5,4},{6,5},{7,6},{8,7},{9,8},{10,9},{11,1... | collective-permute-start | bytes 221192 | tf_op jit(solution)/shard_map/ppermute | solution.py:18
  62.2 7.0 %collective-permute-start.2 = (bf16[1,2,6,1,3072]{4,3,2,1,0:T(2,128)(2,1)S(1)}, bf16[1,2,6,1,3072]{4,3,2,1,0:T(2,128)(2,1)S(1)}, u32[]{:S(2)}, u32[]{:S(2)}) collective-permute-start(bf16[1,2,6,1,3072]{4,3,2,1,0:T(2,128)(2,1)S(1)} %get-tuple-element.91), channel_id=1, source_target_pairs={{0,1},{1,2},{2,3},{3,4},{4,5},{5,6},{6,7},{7,8},{8,9},{9,10},{10,1... | collective-permute-start | bytes 221192 | tf_op jit(solution)/shard_map/ppermute | solution.py:15
  64.2 10.6 %copy-start.3 = (f32[1,3072]{1,0:T(1,128)}, f32[1,3072]{1,0:T(1,128)S(1)}, u32[]{:S(2)}) copy-start(f32[1,3072]{1,0:T(1,128)S(1)} %get-tuple-element.107) | copy-start | bytes 36868
  74.8 84.4 %all-to-all-start = ((bf16[16,1,2,4,4,3072]{5,4,3,2,1,0:T(4,128)(2,1)}), bf16[16,1,2,4,4,3072]{5,4,3,2,1,0:T(4,128)(2,1)S(1)}, u32[]{:S(2)}, u32[]{:S(2)}) async-start(bf16[16,1,2,4,4,3072]{5,4,3,2,1,0:T(4,128)(2,1)} %stack.2), calls=%async_computation | async-start | bytes 6291456 | tf_op jit(solution)/shard_map/all_to_all | solution.py:84
  85.9 83.2 %all-gather.8.cloned.1.call-start = ((), (), s32[]{:S(2)}) async-start(), calls=%async_computation.1 | async-start | bytes 2433024 | tf_op jit(solution)/shard_map/all_gather | solution.py:96
  86.7 165.6 %all-gather.10.cloned.1.call-start = ((), (), s32[]{:S(2)}) async-start(), calls=%async_computation.2 | async-start | bytes 2228224 | tf_op jit(solution)/shard_map/all_gather | solution.py:116
  168.1 7.5 %copy-start.1 = (bf16[1,226,3072]{2,1,0:T(8,128)(2,1)S(1)}, bf16[1,226,3072]{2,1,0:T(8,128)(2,1)}, u32[]{:S(2)}) copy-start(bf16[1,226,3072]{2,1,0:T(8,128)(2,1)} %param.10) | copy-start | bytes 4165636
  173.2 3.1 copy-start.4
  174.0 154.2 %all-gather.12.cloned.1.call-start = ((), (), s32[]{:S(2)}) async-start(), calls=%async_computation.3 | async-start | bytes 2228224 | tf_op jit(solution)/shard_map/all_gather | solution.py:117
  174.7 1.7 copy-start.5
Sparse Core Ops, SparseCore 0:
  88.9 80.2 all-gather.7
  174.1 78.1 all-gather.9
  254.4 73.8 all-gather.11
